TPU v7x, 256 devices: a whole 4x4x8 slice. The times are simulated.
256 devices in a mesh: tgt: 32 (over z, y_hi, core), src: 8 (over y_lo, x).
Axes of the slice: x: 4, y: 4 (y_hi: 2, y_lo: 2; y = y_hi * 2 + y_lo), z: 8, core: 2. Of those that a mesh axis runs over, the one named last changes fastest.
Arguments:
- tgt_points: bfloat16 [3, 16384], P(None, 'tgt'), may hold values from -4 to 4
- tgt_weight: float32 [16384], P('tgt'), may hold values from 0.5 to 2
- src_points: bfloat16 [4, 3, 32768], P(None, None, ('tgt', 'src')), may hold values from -4 to 4
- src_weight: float32 [4, 32768], P(None, ('tgt', 'src')), may hold values from 0.5 to 2
- basis: float32 [4, 3, 32768], P(None, None, ('tgt', 'src')), may hold values from 0.05 to 1
- span: int32 [4, 32768], P(None, ('tgt', 'src')), may hold values from 0 to 29
- patch: int32 [4, 32768], P(None, ('tgt', 'src')), may hold values from 0 to 3
- patch_factor: float32 [4, 2, 1024], P(None, None, ('tgt', 'src')), may hold values from -1.5 to 1.5
- ctrl_weight: float32 [4, 8192], P(None, ('tgt', 'src')), may hold values from 0.5 to 2
- ctrl_coef: bfloat16 [4, 128, 8192], P(None, None, ('tgt', 'src')), may hold values from -6 to 6
- band: float32 [8, 16384], P(None, 'tgt'), may hold values from -0.5 to 0.5
- offsets: int32 [8], replicated, may hold values from -8 to 8, as said below
Outputs:
- shell_field: float32 [16384, 128], P('tgt')
Inputs may be any that keep to these rules, and one draw needn't show every extreme that they name: span of source point j is local to the 32 control points of the block j // 128. patch of source point j is local to the 4 patches of the block j // 128. offsets[0] is 8 and offsets[1] is -8.
All inputs are finite; a program needn't handle non-finite values.
Results may differ from a plain program's by a relative error of at most 0.0041.
Values may be sent and summed in bfloat16 or wider, within the bound.
No kernel may reach another device: no remote copies, remote signals or barrier semaphores. Data moves between devices by JAX's collectives and lax.ppermute only.
A program may use at most 128 MiB of HBM per device.

v0:
```python
import math
import jax
import jax.numpy as jnp
from jax import lax
from jax.sharding import PartitionSpec as P

HALO = 8
WAVE = 8.0
SMOOTH = 0.0025


def extended(block, sides, width):
    for axis, dim in sides:
        count = lax.axis_size(axis)
        forward = [(i, i + 1) for i in range(count - 1)]
        backward = [(target, source) for source, target in forward]
        low = lax.ppermute(
            lax.slice_in_dim(block, block.shape[dim] - width, None, axis=dim), axis, forward
        )
        high = lax.ppermute(lax.slice_in_dim(block, 0, width, axis=dim), axis, backward)
        block = jnp.concatenate([low, block, high], axis=dim)
    return block


def kernel_terms(targets, sources, density):
    tpos = targets.astype(jnp.float32)
    spos = sources.astype(jnp.float32)
    dist_sq = SMOOTH + (tpos[0][:, None] - spos[0][None, :]) ** 2
    dist_sq = dist_sq + (tpos[1][:, None] - spos[1][None, :]) ** 2
    dist_sq = dist_sq + (tpos[2][:, None] - spos[2][None, :]) ** 2
    dist = jnp.sqrt(dist_sq)
    kernel_re = (jnp.cos(WAVE * dist) / dist).astype(jnp.bfloat16)
    kernel_im = (jnp.sin(WAVE * dist) / dist).astype(jnp.bfloat16)
    dims = (((1,), (1,)), ((), ()))
    part_a = lax.dot_general(kernel_re, density, dims, preferred_element_type=jnp.float32)
    part_b = lax.dot_general(kernel_im, density, dims, preferred_element_type=jnp.float32)
    half = density.shape[0] // 2
    return jnp.concatenate(
        [part_a[:, :half] - part_b[:, half:], part_a[:, half:] + part_b[:, :half]], axis=1
    )


def block_density(weight, basis_rows, span_row, patch_row, factor_rows, weights_ctrl, coef_ctrl):
    count = weight.shape[0]
    fields = coef_ctrl.shape[0] // 2
    denom = jnp.zeros((count,), jnp.float32)
    numer = jnp.zeros((coef_ctrl.shape[0], count), jnp.float32)
    for basis_index in range(basis_rows.shape[0]):
        control_index = span_row + basis_index
        scaled = basis_rows[basis_index] * weights_ctrl[control_index]
        denom = denom + scaled
        numer = numer + scaled[None, :] * coef_ctrl[:, control_index].astype(jnp.float32)
    ratio = numer / denom[None, :]
    labels = jnp.arange(factor_rows.shape[1], dtype=jnp.int32)
    member = patch_row[None, :] == labels[:, None]
    factor_re = jnp.sum(jnp.where(member, factor_rows[0][:, None], 0.0), axis=0)
    factor_im = jnp.sum(jnp.where(member, factor_rows[1][:, None], 0.0), axis=0)
    ratio_re = ratio[:fields]
    ratio_im = ratio[fields:]
    dens_re = weight * (factor_re * ratio_re - factor_im * ratio_im)
    dens_im = weight * (factor_re * ratio_im + factor_im * ratio_re)
    return jnp.concatenate([dens_re, dens_im], axis=0).astype(jnp.bfloat16)


def add_kernel(carried, targets, geometry, density):
    width = geometry.shape[1]
    block_size = 1024

    def step_fn(index, inner):
        begin = index * block_size
        part_geo = lax.dynamic_slice_in_dim(geometry, begin, block_size, 1)
        part_den = lax.dynamic_slice_in_dim(density, begin, block_size, 1)
        return inner + kernel_terms(targets, part_geo, part_den)

    return lax.fori_loop(0, width // block_size, step_fn, carried)


def per_device(
    tgt_points,
    tgt_weight,
    src_points,
    src_weight,
    basis,
    span,
    patch,
    patch_factor,
    ctrl_weight,
    ctrl_coef,
    band,
    offsets,
):
    rows = tgt_points.shape[1]
    columns = ctrl_coef.shape[1]
    rounds = src_weight.shape[0]
    partial_value = jnp.zeros((rows, columns), jnp.float32)
    for section in range(rounds):
        density = block_density(
            src_weight[section],
            basis[section],
            span[section],
            patch[section],
            patch_factor[section],
            ctrl_weight[section],
            ctrl_coef[section],
        )
        geometry, gathered = (
            lax.all_gather(src_points[section], "tgt", axis=1, tiled=True),
            lax.all_gather(density, "tgt", axis=1, tiled=True),
        )
        partial_value = add_kernel(partial_value, tgt_points, geometry, gathered)
    total = lax.psum(partial_value, "src")
    source_count = rounds * src_weight.shape[1] * lax.axis_size("tgt") * lax.axis_size("src")
    scale = jnp.float32(1.0 / math.sqrt(source_count))
    potential = total * scale * tgt_weight[:, None]
    padded = extended(potential, (("tgt", 0),), HALO)
    shell_field = potential
    for diag in range(band.shape[0]):
        begin = HALO + offsets[diag]
        shifted = lax.dynamic_slice_in_dim(padded, begin, rows, 0)
        shell_field = shell_field + band[diag][:, None] * shifted
    return shell_field


def solution(mesh):
    in_specs = (
        P(None, "tgt"),
        P("tgt"),
        P(None, None, ("tgt", "src")),
        P(None, ("tgt", "src")),
        P(None, None, ("tgt", "src")),
        P(None, ("tgt", "src")),
        P(None, ("tgt", "src")),
        P(None, None, ("tgt", "src")),
        P(None, ("tgt", "src")),
        P(None, None, ("tgt", "src")),
        P(None, "tgt"),
        P(),
    )
    out_specs = P("tgt", None)
    return jax.shard_map(
        per_device, mesh=mesh, in_specs=in_specs, out_specs=out_specs, check_vma=False
    )
```

profile of v0, /device:TPU:1, one launch (start us, length us, event | category | flops | bytes accessed | tf_op | source)
XLA Modules:
  0.0 627.5 jit_solution(9285904822959095373)
XLA Ops:
  11.6 1.2 gather_fusion.2
  15.2 1.2 gather_fusion.20
  17.7 1.2 gather_fusion.22
  19.0 1.2 gather_fusion.10
  37.3 46.2 %all-gather = bf16[1,3,4096]{2,1,0:T(4,128)(2,1)S(1)} all-gather(bf16[1,3,128]{2,1,0:T(4,128)(2,1)S(1)} %copy.57), channel_id=2, replica_groups=mesh['tgt'=32,'src'=8] {'tgt'}, dimensions={2}, use_global_device_ids=true | all-gather | bytes 25344 | tf_op jit(solution)/shard_map/all_gather | solution.py:107
  83.5 36.7 %all-gather.1 = bf16[1,3,4096]{2,1,0:T(4,128)(2,1)S(1)} all-gather(bf16[1,3,128]{2,1,0:T(4,128)(2,1)S(1)} %copy.58), channel_id=3, replica_groups=mesh['tgt'=32,'src'=8] {'tgt'}, dimensions={2}, use_global_device_ids=true | all-gather | bytes 25344 | tf_op jit(solution)/shard_map/all_gather | solution.py:107
  120.2 39.6 %all-gather.2 = bf16[1,3,4096]{2,1,0:T(4,128)(2,1)S(1)} all-gather(bf16[1,3,128]{2,1,0:T(4,128)(2,1)S(1)} %copy.59), channel_id=4, replica_groups=mesh['tgt'=32,'src'=8] {'tgt'}, dimensions={2}, use_global_device_ids=true | all-gather | bytes 25344 | tf_op jit(solution)/shard_map/all_gather | solution.py:107
  159.8 36.7 %all-gather.3 = bf16[1,3,4096]{2,1,0:T(4,128)(2,1)S(1)} all-gather(bf16[1,3,128]{2,1,0:T(4,128)(2,1)S(1)} %copy.60), channel_id=5, replica_groups=mesh['tgt'=32,'src'=8] {'tgt'}, dimensions={2}, use_global_device_ids=true | all-gather | bytes 25344 | tf_op jit(solution)/shard_map/all_gather | solution.py:107
  196.5 78.8 %while.56 = (s32[]{:T(128)}, f32[512,128]{0,1:T(8,128)S(1)}, bf16[3,512]{1,0:T(4,128)(2,1)S(1)}, bf16[3,4096]{1,0:T(4,128)(2,1)S(1)}, bf16[128,4096]{1,0:T(8,128...) while((s32[]{:T(128)}, f32[512,128]{0,1:T(8,128)S(1)}, bf16[3,512]{1,0:T(4,128)(2,1)S(1)}, ...), condition=%wide.region_3.4_spmd.clone, body=%wide.region_2.3_spmd.clone.sunk | while | flops 281283584 | bytes 2713769 | solution.py:75
  196.7 9.7 %fusion.110 = f32[512,128]{0,1:T(8,128)S(1)} fusion(f32[1024]{0:T(1024)S(1)} %bitcast.278, f32[512]{0:T(512)S(1)} %bitcast.304, f32[1024]{0:T(1024)S(1)} %bitcast.280, f32[512]{0:T(512)S(1)} %bitcast.302, f32[1024]{0:T(1024)S(1)} %bitcast.276, f32[512]{0:T(512)S(1)} %bitcast.300, bf16[128,4096]{1,0:T(8,128)(2,1)} %get-tuple-element.859, ...), kind=kOutput, calls=%fused_computation.79.clone.1 | convolution fusion | flops 140509184 | bytes 542724 | tf_op jit(solution)/shard_map/while/body/eval_jaxpr/dot_general | solution.py:36
  206.4 9.6 %fusion.111 = f32[512,128]{0,1:T(8,128)S(1)} fusion(f32[1024]{0:T(1024)S(1)} %bitcast.279, f32[512]{0:T(512)S(1)} %bitcast.305, f32[1024]{0:T(1024)S(1)} %bitcast.281, f32[512]{0:T(512)S(1)} %bitcast.303, f32[1024]{0:T(1024)S(1)} %bitcast.277, f32[512]{0:T(512)S(1)} %bitcast.301, bf16[128,4096]{1,0:T(8,128)(2,1)} %get-tuple-element.859, ...), kind=kOutput, calls=%fused_computation.78.clone.1 | convolution fusion | flops 140509184 | bytes 542724 | tf_op jit(solution)/shard_map/while/body/eval_jaxpr/dot_general | solution.py:35
  216.3 9.7 %fusion.110 = f32[512,128]{0,1:T(8,128)S(1)} fusion(f32[1024]{0:T(1024)S(1)} %bitcast.278, f32[512]{0:T(512)S(1)} %bitcast.304, f32[1024]{0:T(1024)S(1)} %bitcast.280, f32[512]{0:T(512)S(1)} %bitcast.302, f32[1024]{0:T(1024)S(1)} %bitcast.276, f32[512]{0:T(512)S(1)} %bitcast.300, bf16[128,4096]{1,0:T(8,128)(2,1)} %get-tuple-element.859, ...), kind=kOutput, calls=%fused_computation.79.clone.1 | convolution fusion | flops 140509184 | bytes 542724 | tf_op jit(solution)/shard_map/while/body/eval_jaxpr/dot_general | solution.py:36
  226.0 9.6 %fusion.111 = f32[512,128]{0,1:T(8,128)S(1)} fusion(f32[1024]{0:T(1024)S(1)} %bitcast.279, f32[512]{0:T(512)S(1)} %bitcast.305, f32[1024]{0:T(1024)S(1)} %bitcast.281, f32[512]{0:T(512)S(1)} %bitcast.303, f32[1024]{0:T(1024)S(1)} %bitcast.277, f32[512]{0:T(512)S(1)} %bitcast.301, bf16[128,4096]{1,0:T(8,128)(2,1)} %get-tuple-element.859, ...), kind=kOutput, calls=%fused_computation.78.clone.1 | convolution fusion | flops 140509184 | bytes 542724 | tf_op jit(solution)/shard_map/while/body/eval_jaxpr/dot_general | solution.py:35
  235.8 9.7 %fusion.110 = f32[512,128]{0,1:T(8,128)S(1)} fusion(f32[1024]{0:T(1024)S(1)} %bitcast.278, f32[512]{0:T(512)S(1)} %bitcast.304, f32[1024]{0:T(1024)S(1)} %bitcast.280, f32[512]{0:T(512)S(1)} %bitcast.302, f32[1024]{0:T(1024)S(1)} %bitcast.276, f32[512]{0:T(512)S(1)} %bitcast.300, bf16[128,4096]{1,0:T(8,128)(2,1)} %get-tuple-element.859, ...), kind=kOutput, calls=%fused_computation.79.clone.1 | convolution fusion | flops 140509184 | bytes 542724 | tf_op jit(solution)/shard_map/while/body/eval_jaxpr/dot_general | solution.py:36
  245.5 9.6 %fusion.111 = f32[512,128]{0,1:T(8,128)S(1)} fusion(f32[1024]{0:T(1024)S(1)} %bitcast.279, f32[512]{0:T(512)S(1)} %bitcast.305, f32[1024]{0:T(1024)S(1)} %bitcast.281, f32[512]{0:T(512)S(1)} %bitcast.303, f32[1024]{0:T(1024)S(1)} %bitcast.277, f32[512]{0:T(512)S(1)} %bitcast.301, bf16[128,4096]{1,0:T(8,128)(2,1)} %get-tuple-element.859, ...), kind=kOutput, calls=%fused_computation.78.clone.1 | convolution fusion | flops 140509184 | bytes 542724 | tf_op jit(solution)/shard_map/while/body/eval_jaxpr/dot_general | solution.py:35
  255.4 9.7 %fusion.110 = f32[512,128]{0,1:T(8,128)S(1)} fusion(f32[1024]{0:T(1024)S(1)} %bitcast.278, f32[512]{0:T(512)S(1)} %bitcast.304, f32[1024]{0:T(1024)S(1)} %bitcast.280, f32[512]{0:T(512)S(1)} %bitcast.302, f32[1024]{0:T(1024)S(1)} %bitcast.276, f32[512]{0:T(512)S(1)} %bitcast.300, bf16[128,4096]{1,0:T(8,128)(2,1)} %get-tuple-element.859, ...), kind=kOutput, calls=%fused_computation.79.clone.1 | convolution fusion | flops 140509184 | bytes 542724 | tf_op jit(solution)/shard_map/while/body/eval_jaxpr/dot_general | solution.py:36
  265.1 9.6 %fusion.111 = f32[512,128]{0,1:T(8,128)S(1)} fusion(f32[1024]{0:T(1024)S(1)} %bitcast.279, f32[512]{0:T(512)S(1)} %bitcast.305, f32[1024]{0:T(1024)S(1)} %bitcast.281, f32[512]{0:T(512)S(1)} %bitcast.303, f32[1024]{0:T(1024)S(1)} %bitcast.277, f32[512]{0:T(512)S(1)} %bitcast.301, bf16[128,4096]{1,0:T(8,128)(2,1)} %get-tuple-element.859, ...), kind=kOutput, calls=%fused_computation.78.clone.1 | convolution fusion | flops 140509184 | bytes 542724 | tf_op jit(solution)/shard_map/while/body/eval_jaxpr/dot_general | solution.py:35
  275.3 78.1 %while.53 = (s32[]{:T(128)}, f32[512,128]{0,1:T(8,128)S(1)}, bf16[3,512]{1,0:T(4,128)(2,1)S(1)}, bf16[3,4096]{1,0:T(4,128)(2,1)S(1)}, bf16[128,4096]{1,0:T(8,128...) while((s32[]{:T(128)}, f32[512,128]{0,1:T(8,128)S(1)}, bf16[3,512]{1,0:T(4,128)(2,1)S(1)}, ...), condition=%wide.region_7.8_spmd, body=%wide.region_6.7_spmd.sunk | while | flops 281218048 | bytes 2713759 | solution.py:75
  275.4 9.7 %fusion.92 = f32[512,128]{0,1:T(8,128)S(1)} fusion(f32[1024]{0:T(1024)S(1)} %bitcast.284, f32[512]{0:T(512)S(1)} %bitcast.310, f32[1024]{0:T(1024)S(1)} %bitcast.286, f32[512]{0:T(512)S(1)} %bitcast.308, f32[1024]{0:T(1024)S(1)} %bitcast.282, f32[512]{0:T(512)S(1)} %bitcast.306, bf16[128,4096]{1,0:T(8,128)(2,1)} %get-tuple-element.886, ...), kind=kOutput, calls=%fused_computation.28.clone.1 | convolution fusion | flops 140509184 | bytes 542724 | tf_op jit(solution)/shard_map/while/body/eval_jaxpr/dot_general | solution.py:36
  285.1 9.6 %fusion.93 = f32[512,128]{0,1:T(8,128)S(1)} fusion(f32[1024]{0:T(1024)S(1)} %bitcast.285, f32[512]{0:T(512)S(1)} %bitcast.311, f32[1024]{0:T(1024)S(1)} %bitcast.287, f32[512]{0:T(512)S(1)} %bitcast.309, f32[1024]{0:T(1024)S(1)} %bitcast.283, f32[512]{0:T(512)S(1)} %bitcast.307, bf16[128,4096]{1,0:T(8,128)(2,1)} %get-tuple-element.886, ...), kind=kOutput, calls=%fused_computation.27.clone.1 | convolution fusion | flops 140509184 | bytes 542724 | tf_op jit(solution)/shard_map/while/body/eval_jaxpr/dot_general | solution.py:35
  294.9 9.7 %fusion.92 = f32[512,128]{0,1:T(8,128)S(1)} fusion(f32[1024]{0:T(1024)S(1)} %bitcast.284, f32[512]{0:T(512)S(1)} %bitcast.310, f32[1024]{0:T(1024)S(1)} %bitcast.286, f32[512]{0:T(512)S(1)} %bitcast.308, f32[1024]{0:T(1024)S(1)} %bitcast.282, f32[512]{0:T(512)S(1)} %bitcast.306, bf16[128,4096]{1,0:T(8,128)(2,1)} %get-tuple-element.886, ...), kind=kOutput, calls=%fused_computation.28.clone.1 | convolution fusion | flops 140509184 | bytes 542724 | tf_op jit(solution)/shard_map/while/body/eval_jaxpr/dot_general | solution.py:36
  304.6 9.6 %fusion.93 = f32[512,128]{0,1:T(8,128)S(1)} fusion(f32[1024]{0:T(1024)S(1)} %bitcast.285, f32[512]{0:T(512)S(1)} %bitcast.311, f32[1024]{0:T(1024)S(1)} %bitcast.287, f32[512]{0:T(512)S(1)} %bitcast.309, f32[1024]{0:T(1024)S(1)} %bitcast.283, f32[512]{0:T(512)S(1)} %bitcast.307, bf16[128,4096]{1,0:T(8,128)(2,1)} %get-tuple-element.886, ...), kind=kOutput, calls=%fused_computation.27.clone.1 | convolution fusion | flops 140509184 | bytes 542724 | tf_op jit(solution)/shard_map/while/body/eval_jaxpr/dot_general | solution.py:35
  314.5 9.7 %fusion.92 = f32[512,128]{0,1:T(8,128)S(1)} fusion(f32[1024]{0:T(1024)S(1)} %bitcast.284, f32[512]{0:T(512)S(1)} %bitcast.310, f32[1024]{0:T(1024)S(1)} %bitcast.286, f32[512]{0:T(512)S(1)} %bitcast.308, f32[1024]{0:T(1024)S(1)} %bitcast.282, f32[512]{0:T(512)S(1)} %bitcast.306, bf16[128,4096]{1,0:T(8,128)(2,1)} %get-tuple-element.886, ...), kind=kOutput, calls=%fused_computation.28.clone.1 | convolution fusion | flops 140509184 | bytes 542724 | tf_op jit(solution)/shard_map/while/body/eval_jaxpr/dot_general | solution.py:36
  324.1 9.6 %fusion.93 = f32[512,128]{0,1:T(8,128)S(1)} fusion(f32[1024]{0:T(1024)S(1)} %bitcast.285, f32[512]{0:T(512)S(1)} %bitcast.311, f32[1024]{0:T(1024)S(1)} %bitcast.287, f32[512]{0:T(512)S(1)} %bitcast.309, f32[1024]{0:T(1024)S(1)} %bitcast.283, f32[512]{0:T(512)S(1)} %bitcast.307, bf16[128,4096]{1,0:T(8,128)(2,1)} %get-tuple-element.886, ...), kind=kOutput, calls=%fused_computation.27.clone.1 | convolution fusion | flops 140509184 | bytes 542724 | tf_op jit(solution)/shard_map/while/body/eval_jaxpr/dot_general | solution.py:35
  334.0 9.7 %fusion.92 = f32[512,128]{0,1:T(8,128)S(1)} fusion(f32[1024]{0:T(1024)S(1)} %bitcast.284, f32[512]{0:T(512)S(1)} %bitcast.310, f32[1024]{0:T(1024)S(1)} %bitcast.286, f32[512]{0:T(512)S(1)} %bitcast.308, f32[1024]{0:T(1024)S(1)} %bitcast.282, f32[512]{0:T(512)S(1)} %bitcast.306, bf16[128,4096]{1,0:T(8,128)(2,1)} %get-tuple-element.886, ...), kind=kOutput, calls=%fused_computation.28.clone.1 | convolution fusion | flops 140509184 | bytes 542724 | tf_op jit(solution)/shard_map/while/body/eval_jaxpr/dot_general | solution.py:36
  343.7 9.6 %fusion.93 = f32[512,128]{0,1:T(8,128)S(1)} fusion(f32[1024]{0:T(1024)S(1)} %bitcast.285, f32[512]{0:T(512)S(1)} %bitcast.311, f32[1024]{0:T(1024)S(1)} %bitcast.287, f32[512]{0:T(512)S(1)} %bitcast.309, f32[1024]{0:T(1024)S(1)} %bitcast.283, f32[512]{0:T(512)S(1)} %bitcast.307, bf16[128,4096]{1,0:T(8,128)(2,1)} %get-tuple-element.886, ...), kind=kOutput, calls=%fused_computation.27.clone.1 | convolution fusion | flops 140509184 | bytes 542724 | tf_op jit(solution)/shard_map/while/body/eval_jaxpr/dot_general | solution.py:35
  353.5 78.3 %while.54 = (s32[]{:T(128)}, f32[512,128]{0,1:T(8,128)S(1)}, bf16[3,512]{1,0:T(4,128)(2,1)S(1)}, bf16[3,4096]{1,0:T(4,128)(2,1)S(1)}, bf16[128,4096]{1,0:T(8,128...) while((s32[]{:T(128)}, f32[512,128]{0,1:T(8,128)S(1)}, bf16[3,512]{1,0:T(4,128)(2,1)S(1)}, ...), condition=%wide.region_11.12_spmd, body=%wide.region_10.11_spmd.sunk | while | flops 281218048 | bytes 2713759 | solution.py:75
  353.7 9.7 %fusion.98 = f32[512,128]{0,1:T(8,128)S(1)} fusion(f32[1024]{0:T(1024)S(1)} %bitcast.290, f32[512]{0:T(512)S(1)} %bitcast.316, f32[1024]{0:T(1024)S(1)} %bitcast.292, f32[512]{0:T(512)S(1)} %bitcast.314, f32[1024]{0:T(1024)S(1)} %bitcast.288, f32[512]{0:T(512)S(1)} %bitcast.312, bf16[128,4096]{1,0:T(8,128)(2,1)} %get-tuple-element.913, ...), kind=kOutput, calls=%fused_computation.45.clone.1 | convolution fusion | flops 140509184 | bytes 542724 | tf_op jit(solution)/shard_map/while/body/eval_jaxpr/dot_general | solution.py:36
  363.4 9.6 %fusion.99 = f32[512,128]{0,1:T(8,128)S(1)} fusion(f32[1024]{0:T(1024)S(1)} %bitcast.291, f32[512]{0:T(512)S(1)} %bitcast.317, f32[1024]{0:T(1024)S(1)} %bitcast.293, f32[512]{0:T(512)S(1)} %bitcast.315, f32[1024]{0:T(1024)S(1)} %bitcast.289, f32[512]{0:T(512)S(1)} %bitcast.313, bf16[128,4096]{1,0:T(8,128)(2,1)} %get-tuple-element.913, ...), kind=kOutput, calls=%fused_computation.44.clone.1 | convolution fusion | flops 140509184 | bytes 542724 | tf_op jit(solution)/shard_map/while/body/eval_jaxpr/dot_general | solution.py:35
  373.3 9.7 %fusion.98 = f32[512,128]{0,1:T(8,128)S(1)} fusion(f32[1024]{0:T(1024)S(1)} %bitcast.290, f32[512]{0:T(512)S(1)} %bitcast.316, f32[1024]{0:T(1024)S(1)} %bitcast.292, f32[512]{0:T(512)S(1)} %bitcast.314, f32[1024]{0:T(1024)S(1)} %bitcast.288, f32[512]{0:T(512)S(1)} %bitcast.312, bf16[128,4096]{1,0:T(8,128)(2,1)} %get-tuple-element.913, ...), kind=kOutput, calls=%fused_computation.45.clone.1 | convolution fusion | flops 140509184 | bytes 542724 | tf_op jit(solution)/shard_map/while/body/eval_jaxpr/dot_general | solution.py:36
  383.0 9.6 %fusion.99 = f32[512,128]{0,1:T(8,128)S(1)} fusion(f32[1024]{0:T(1024)S(1)} %bitcast.291, f32[512]{0:T(512)S(1)} %bitcast.317, f32[1024]{0:T(1024)S(1)} %bitcast.293, f32[512]{0:T(512)S(1)} %bitcast.315, f32[1024]{0:T(1024)S(1)} %bitcast.289, f32[512]{0:T(512)S(1)} %bitcast.313, bf16[128,4096]{1,0:T(8,128)(2,1)} %get-tuple-element.913, ...), kind=kOutput, calls=%fused_computation.44.clone.1 | convolution fusion | flops 140509184 | bytes 542724 | tf_op jit(solution)/shard_map/while/body/eval_jaxpr/dot_general | solution.py:35
  392.8 9.7 %fusion.98 = f32[512,128]{0,1:T(8,128)S(1)} fusion(f32[1024]{0:T(1024)S(1)} %bitcast.290, f32[512]{0:T(512)S(1)} %bitcast.316, f32[1024]{0:T(1024)S(1)} %bitcast.292, f32[512]{0:T(512)S(1)} %bitcast.314, f32[1024]{0:T(1024)S(1)} %bitcast.288, f32[512]{0:T(512)S(1)} %bitcast.312, bf16[128,4096]{1,0:T(8,128)(2,1)} %get-tuple-element.913, ...), kind=kOutput, calls=%fused_computation.45.clone.1 | convolution fusion | flops 140509184 | bytes 542724 | tf_op jit(solution)/shard_map/while/body/eval_jaxpr/dot_general | solution.py:36
  402.5 9.6 %fusion.99 = f32[512,128]{0,1:T(8,128)S(1)} fusion(f32[1024]{0:T(1024)S(1)} %bitcast.291, f32[512]{0:T(512)S(1)} %bitcast.317, f32[1024]{0:T(1024)S(1)} %bitcast.293, f32[512]{0:T(512)S(1)} %bitcast.315, f32[1024]{0:T(1024)S(1)} %bitcast.289, f32[512]{0:T(512)S(1)} %bitcast.313, bf16[128,4096]{1,0:T(8,128)(2,1)} %get-tuple-element.913, ...), kind=kOutput, calls=%fused_computation.44.clone.1 | convolution fusion | flops 140509184 | bytes 542724 | tf_op jit(solution)/shard_map/while/body/eval_jaxpr/dot_general | solution.py:35
  412.3 9.7 %fusion.98 = f32[512,128]{0,1:T(8,128)S(1)} fusion(f32[1024]{0:T(1024)S(1)} %bitcast.290, f32[512]{0:T(512)S(1)} %bitcast.316, f32[1024]{0:T(1024)S(1)} %bitcast.292, f32[512]{0:T(512)S(1)} %bitcast.314, f32[1024]{0:T(1024)S(1)} %bitcast.288, f32[512]{0:T(512)S(1)} %bitcast.312, bf16[128,4096]{1,0:T(8,128)(2,1)} %get-tuple-element.913, ...), kind=kOutput, calls=%fused_computation.45.clone.1 | convolution fusion | flops 140509184 | bytes 542724 | tf_op jit(solution)/shard_map/while/body/eval_jaxpr/dot_general | solution.py:36
  422.0 9.6 %fusion.99 = f32[512,128]{0,1:T(8,128)S(1)} fusion(f32[1024]{0:T(1024)S(1)} %bitcast.291, f32[512]{0:T(512)S(1)} %bitcast.317, f32[1024]{0:T(1024)S(1)} %bitcast.293, f32[512]{0:T(512)S(1)} %bitcast.315, f32[1024]{0:T(1024)S(1)} %bitcast.289, f32[512]{0:T(512)S(1)} %bitcast.313, bf16[128,4096]{1,0:T(8,128)(2,1)} %get-tuple-element.913, ...), kind=kOutput, calls=%fused_computation.44.clone.1 | convolution fusion | flops 140509184 | bytes 542724 | tf_op jit(solution)/shard_map/while/body/eval_jaxpr/dot_general | solution.py:35
  431.8 91.2 %while.55 = (s32[]{:T(128)}, f32[512,128]{0,1:T(8,128)S(1)}, bf16[3,512]{1,0:T(4,128)(2,1)S(1)}, bf16[3,4096]{1,0:T(4,128)(2,1)S(1)}, bf16[128,4096]{1,0:T(8,128...) while((s32[]{:T(128)}, f32[512,128]{0,1:T(8,128)S(1)}, bf16[3,512]{1,0:T(4,128)(2,1)S(1)}, ...), condition=%wide.region_15.16_spmd, body=%wide.region_14.15_spmd.sunk | while | flops 281218048 | bytes 2713759 | solution.py:75
  445.0 9.7 %fusion.104 = f32[512,128]{0,1:T(8,128)S(1)} fusion(f32[1024]{0:T(1024)S(1)} %bitcast.296, f32[512]{0:T(512)S(1)} %bitcast.322, f32[1024]{0:T(1024)S(1)} %bitcast.298, f32[512]{0:T(512)S(1)} %bitcast.320, f32[1024]{0:T(1024)S(1)} %bitcast.294, f32[512]{0:T(512)S(1)} %bitcast.318, bf16[128,4096]{1,0:T(8,128)(2,1)} %get-tuple-element.940, ...), kind=kOutput, calls=%fused_computation.62.clone.1 | convolution fusion | flops 140509184 | bytes 542724 | tf_op jit(solution)/shard_map/while/body/eval_jaxpr/dot_general | solution.py:36
  454.7 9.6 %fusion.105 = f32[512,128]{0,1:T(8,128)S(1)} fusion(f32[1024]{0:T(1024)S(1)} %bitcast.297, f32[512]{0:T(512)S(1)} %bitcast.323, f32[1024]{0:T(1024)S(1)} %bitcast.299, f32[512]{0:T(512)S(1)} %bitcast.321, f32[1024]{0:T(1024)S(1)} %bitcast.295, f32[512]{0:T(512)S(1)} %bitcast.319, bf16[128,4096]{1,0:T(8,128)(2,1)} %get-tuple-element.940, ...), kind=kOutput, calls=%fused_computation.61.clone.1 | convolution fusion | flops 140509184 | bytes 542724 | tf_op jit(solution)/shard_map/while/body/eval_jaxpr/dot_general | solution.py:35
  464.5 9.7 %fusion.104 = f32[512,128]{0,1:T(8,128)S(1)} fusion(f32[1024]{0:T(1024)S(1)} %bitcast.296, f32[512]{0:T(512)S(1)} %bitcast.322, f32[1024]{0:T(1024)S(1)} %bitcast.298, f32[512]{0:T(512)S(1)} %bitcast.320, f32[1024]{0:T(1024)S(1)} %bitcast.294, f32[512]{0:T(512)S(1)} %bitcast.318, bf16[128,4096]{1,0:T(8,128)(2,1)} %get-tuple-element.940, ...), kind=kOutput, calls=%fused_computation.62.clone.1 | convolution fusion | flops 140509184 | bytes 542724 | tf_op jit(solution)/shard_map/while/body/eval_jaxpr/dot_general | solution.py:36
  474.2 9.6 %fusion.105 = f32[512,128]{0,1:T(8,128)S(1)} fusion(f32[1024]{0:T(1024)S(1)} %bitcast.297, f32[512]{0:T(512)S(1)} %bitcast.323, f32[1024]{0:T(1024)S(1)} %bitcast.299, f32[512]{0:T(512)S(1)} %bitcast.321, f32[1024]{0:T(1024)S(1)} %bitcast.295, f32[512]{0:T(512)S(1)} %bitcast.319, bf16[128,4096]{1,0:T(8,128)(2,1)} %get-tuple-element.940, ...), kind=kOutput, calls=%fused_computation.61.clone.1 | convolution fusion | flops 140509184 | bytes 542724 | tf_op jit(solution)/shard_map/while/body/eval_jaxpr/dot_general | solution.py:35
  484.1 9.7 %fusion.104 = f32[512,128]{0,1:T(8,128)S(1)} fusion(f32[1024]{0:T(1024)S(1)} %bitcast.296, f32[512]{0:T(512)S(1)} %bitcast.322, f32[1024]{0:T(1024)S(1)} %bitcast.298, f32[512]{0:T(512)S(1)} %bitcast.320, f32[1024]{0:T(1024)S(1)} %bitcast.294, f32[512]{0:T(512)S(1)} %bitcast.318, bf16[128,4096]{1,0:T(8,128)(2,1)} %get-tuple-element.940, ...), kind=kOutput, calls=%fused_computation.62.clone.1 | convolution fusion | flops 140509184 | bytes 542724 | tf_op jit(solution)/shard_map/while/body/eval_jaxpr/dot_general | solution.py:36
  493.8 9.6 %fusion.105 = f32[512,128]{0,1:T(8,128)S(1)} fusion(f32[1024]{0:T(1024)S(1)} %bitcast.297, f32[512]{0:T(512)S(1)} %bitcast.323, f32[1024]{0:T(1024)S(1)} %bitcast.299, f32[512]{0:T(512)S(1)} %bitcast.321, f32[1024]{0:T(1024)S(1)} %bitcast.295, f32[512]{0:T(512)S(1)} %bitcast.319, bf16[128,4096]{1,0:T(8,128)(2,1)} %get-tuple-element.940, ...), kind=kOutput, calls=%fused_computation.61.clone.1 | convolution fusion | flops 140509184 | bytes 542724 | tf_op jit(solution)/shard_map/while/body/eval_jaxpr/dot_general | solution.py:35
  503.6 9.7 %fusion.104 = f32[512,128]{0,1:T(8,128)S(1)} fusion(f32[1024]{0:T(1024)S(1)} %bitcast.296, f32[512]{0:T(512)S(1)} %bitcast.322, f32[1024]{0:T(1024)S(1)} %bitcast.298, f32[512]{0:T(512)S(1)} %bitcast.320, f32[1024]{0:T(1024)S(1)} %bitcast.294, f32[512]{0:T(512)S(1)} %bitcast.318, bf16[128,4096]{1,0:T(8,128)(2,1)} %get-tuple-element.940, ...), kind=kOutput, calls=%fused_computation.62.clone.1 | convolution fusion | flops 140509184 | bytes 542724 | tf_op jit(solution)/shard_map/while/body/eval_jaxpr/dot_general | solution.py:36
  513.3 9.6 %fusion.105 = f32[512,128]{0,1:T(8,128)S(1)} fusion(f32[1024]{0:T(1024)S(1)} %bitcast.297, f32[512]{0:T(512)S(1)} %bitcast.323, f32[1024]{0:T(1024)S(1)} %bitcast.299, f32[512]{0:T(512)S(1)} %bitcast.321, f32[1024]{0:T(1024)S(1)} %bitcast.295, f32[512]{0:T(512)S(1)} %bitcast.319, bf16[128,4096]{1,0:T(8,128)(2,1)} %get-tuple-element.940, ...), kind=kOutput, calls=%fused_computation.61.clone.1 | convolution fusion | flops 140509184 | bytes 542724 | tf_op jit(solution)/shard_map/while/body/eval_jaxpr/dot_general | solution.py:35
  524.0 71.3 %all-reduce.2.cloned.1.call-done = f32[512,128]{1,0:T(8,128)} async-done(((f32[512,128]{1,0:T(8,128)}), f32[512,128]{1,0:T(8,128)}) %all-reduce.2.cloned.1.call-update) | async-done | bytes 262160 | tf_op jit(solution)/shard_map/psum | solution.py:111
  596.5 7.5 %collective-permute-start.1 = (f32[8,128]{1,0:T(8,128)S(1)}, f32[8,128]{1,0:T(8,128)S(1)}, u32[]{:S(2)}, u32[]{:S(2)}) collective-permute-start(f32[8,128]{1,0:T(8,128)S(1)} %get-tuple-element.560), channel_id=1, source_target_pairs={{8,0},{16,8},{24,16},{32,24},{40,32},{48,40},{56,48},{64,56},{72,6... | collective-permute-start | bytes 12296 | tf_op jit(solution)/shard_map/ppermute | solution.py:20
  604.0 4.2 collective-permute-start
  619.2 1.6 multiply_add_fusion
  (189 shorter events, 30.5 us)
Async XLA Ops:
  6.5 190.0 %all-gather.9.cloned.1.call-start = ((), (), s32[]{:S(2)}) async-start(), calls=%async_computation | async-start | bytes 1081344 | tf_op jit(solution)/shard_map/all_gather | solution.py:108
  17.7 5.0 copy-start.6
  17.7 5.0 copy-start.7
  17.7 5.0 copy-start.8
  17.7 5.1 copy-start.5
  23.6 251.7 %all-gather.11.cloned.1.call-start = ((), (), s32[]{:S(2)}) async-start(), calls=%async_computation.1 | async-start | bytes 1081344 | tf_op jit(solution)/shard_map/all_gather | solution.py:108
  26.8 326.6 %all-gather.13.cloned.1.call-start = ((), (), s32[]{:S(2)}) async-start(), calls=%async_computation.2 | async-start | bytes 1081344 | tf_op jit(solution)/shard_map/all_gather | solution.py:108
  32.7 4.5 copy-start.4
  33.0 163.5 %copy-start = (bf16[3,512]{1,0:T(4,128)(2,1)S(1)}, bf16[3,512]{1,0:T(4,128)(2,1)}, u32[]{:S(2)}) copy-start(bf16[3,512]{1,0:T(4,128)(2,1)} %param.20) | copy-start | bytes 9220
  33.9 397.9 %all-gather.15.cloned.1.call-start = ((), (), s32[]{:S(2)}) async-start(), calls=%async_computation.3 | async-start | bytes 1081344 | tf_op jit(solution)/shard_map/all_gather | solution.py:108
  37.2 558.2 %all-reduce.2.cloned.1.call-start = ((), (), s32[]{:S(2)}) async-start(), calls=%async_computation.4 | async-start | bytes 524288 | tf_op jit(solution)/shard_map/psum | solution.py:111
  431.8 92.1 %copy-start.9 = (f32[512]{0:T(512)S(1)}, f32[512]{0:T(512)}, u32[]{:S(2)}) copy-start(f32[512]{0:T(512)} %param.21) | copy-start | bytes 6148
  431.8 92.1 %copy-start.3 = (f32[8,512]{1,0:T(8,128)S(1)}, f32[8,512]{1,0:T(8,128)}, u32[]{:S(2)}) copy-start(f32[8,512]{1,0:T(8,128)} %param.30) | copy-start | bytes 49156
  523.1 85.2 %copy-start.2 = (s32[8]{0:T(128)S(1)}, s32[8]{0:T(128)}, u32[]{:S(2)}) copy-start(s32[8]{0:T(128)} %param.31) | copy-start | bytes 100
  595.3 23.9 %copy-start.1 = (f32[512,128]{1,0:T(8,128)S(1)}, f32[512,128]{1,0:T(8,128)}, u32[]{:S(2)}) copy-start(f32[512,128]{1,0:T(8,128)} %all-reduce.2.cloned.1.call-done) | copy-start | bytes 786436
  596.5 22.7 %collective-permute-start.1 = (f32[8,128]{1,0:T(8,128)S(1)}, f32[8,128]{1,0:T(8,128)S(1)}, u32[]{:S(2)}, u32[]{:S(2)}) collective-permute-start(f32[8,128]{1,0:T(8,128)S(1)} %get-tuple-element.560), channel_id=1, source_target_pairs={{8,0},{16,8},{24,16},{32,24},{40,32},{48,40},{56,48},{64,56},{72,6... | collective-permute-start | bytes 12296 | tf_op jit(solution)/shard_map/ppermute | solution.py:20
  604.0 15.2 %collective-permute-start = (f32[8,128]{1,0:T(8,128)S(1)}, f32[8,128]{1,0:T(8,128)S(1)}, u32[]{:S(2)}, u32[]{:S(2)}) collective-permute-start(f32[8,128]{1,0:T(8,128)S(1)} %get-tuple-element.559), channel_id=1, source_target_pairs={{0,8},{8,16},{16,24},{24,32},{32,40},{40,48},{48,56},{56,64},{64,7... | collective-permute-start | bytes 12296 | tf_op jit(solution)/shard_map/ppermute | solution.py:17
Sparse Core Ops, SparseCore 0:
  23.7 76.4 all-gather.8
  102.7 70.0 all-gather.10
  175.4 69.8 all-gather.12
  247.7 69.9 all-gather.14
  524.1 71.2 all-reduce.1
where the time goes:
time: 635 us; the launch traced here: 628 us
  matrix products  309 us (49%)
  blocking collectives  159 us (25%)
  waiting for transfers between devices  71.5 us (11%)
  local copies, waits for them, and re-layouts  28.2 us (4%)
  between operations  24.2 us (4%)
  loops' own time  15.1 us (2%)
  starting transfers between devices  11.9 us (2%)
  other arithmetic  8.44 us (1%)
    all_gather x4, blocking collectives, per_device(): lax.all_gather(src_points[section], 'tgt', axis=1, tiled=True)  159 us
    dot_general x16, matrix products, kernel_terms(): lax.dot_general(kernel_im, density, dims, preferred_element_type=jnp.floa...  155 us
    dot_general x16, matrix products, kernel_terms(): lax.dot_general(kernel_re, density, dims, preferred_element_type=jnp.floa...  154 us
    psum x1, waiting for transfers between devices, per_device(): total = lax.psum(partial_value, 'src')  71.3 us
    another operation x4, loops' own time, add_kernel(): return lax.fori_loop(0, width // block_size, step_fn, carried)  15.1 us
    gather x12, local copies, waits for them, and re-layouts, block_density(): scaled = basis_rows[basis_index] * weights_ctrl[control_index]  14.7 us
  transfers between devices with their start and end apart: 7, of which 1 were waited for; matrix products, arithmetic and copies ran while one was open for 39% of the time, Pallas kernels for 0%

commit v1 on v0

--- a/solution.py
+++ b/solution.py
@@ -104,7 +104,12 @@
             ctrl_coef[section],
         )
         geometry, gathered = (
-            lax.all_gather(src_points[section], "tgt", axis=1, tiled=True),
+            jnp.concatenate(
+                lax.all_to_all(
+                    jnp.stack([src_points[section]] * lax.axis_size("tgt")), "tgt", 0, 0
+                ),
+                axis=1,
+            ),
             lax.all_gather(density, "tgt", axis=1, tiled=True),
         )
         partial_value = add_kernel(partial_value, tgt_points, geometry, gathered)

time: 635 us -> 585 us (0.921)
  blocking collectives: 159 us -> 0 us
  waiting for transfers between devices: 71.5 us -> 120 us
  starting transfers between devices: 11.9 us -> 44.9 us
  loops' own time: 15.1 us -> 40.1 us
    all_gather x4 -> x0, blocking collectives: 159 us -> none  [per_device(): lax.all_gather(src_points[section], 'tgt', axis=1, tiled=True)]
    all_gather x4, waiting for transfers between devices: 0.06 us -> 38.5 us  [per_device(): lax.all_gather(density, 'tgt', axis=1, tiled=True)]
    all_to_all x0 -> x4, starting transfers between devices: none -> 33 us  [per_device(): lax.all_to_all(jnp.stack([src_points[section]] * lax.axis_size('tgt')), '...]
    another operation x4, loops' own time: 15.1 us -> 40.1 us  [add_kernel(): return lax.fori_loop(0, width // block_size, step_fn, carried)]
  transfers between devices with their start and end apart: 7 -> 11, of which waited for: 1 -> 3; matrix products, arithmetic and copies ran while one was open for 39% -> 43% of each run, Pallas kernels for 0% -> 0%
where the time goes in v1:
time: 585 us; the launch traced here: 577 us
  matrix products  309 us (53%)
  waiting for transfers between devices  120 us (21%)
  starting transfers between devices  44.9 us (8%)
  loops' own time  40.1 us (7%)
  local copies, waits for them, and re-layouts  30.7 us (5%)
  between operations  24.1 us (4%)
  other arithmetic  8.42 us (1%)
    dot_general x16, matrix products, kernel_terms(): lax.dot_general(kernel_im, density, dims, preferred_element_type=jnp.floa...  155 us
    dot_general x16, matrix products, kernel_terms(): lax.dot_general(kernel_re, density, dims, preferred_element_type=jnp.floa...  154 us
    psum x1, waiting for transfers between devices, per_device(): total = lax.psum(partial_value, 'src')  74.9 us
    another operation x4, loops' own time, add_kernel(): return lax.fori_loop(0, width // block_size, step_fn, carried)  40.1 us
    all_gather x4, waiting for transfers between devices, per_device(): lax.all_gather(density, 'tgt', axis=1, tiled=True)  38.5 us
    all_to_all x4, starting transfers between devices, per_device(): lax.all_to_all(jnp.stack([src_points[section]] * lax.axis_size('tgt')), '...  33 us
    gather x12, local copies, waits for them, and re-layouts, block_density(): scaled = basis_rows[basis_index] * weights_ctrl[control_index]  14.7 us
  transfers between devices with their start and end apart: 11, of which 3 were waited for; matrix products, arithmetic and copies ran while one was open for 43% of the time, Pallas kernels for 0%

profile of v1, /device:TPU:1, one launch (start us, length us, event | category | flops | bytes accessed | tf_op | source)
XLA Modules:
  0.0 577.2 jit_solution(1185861934704539967)
XLA Ops:
  11.6 1.2 gather_fusion.2
  15.2 1.2 gather_fusion.20
  34.6 12.7 %all-to-all-start = ((bf16[32,3,128]{2,1,0:T(4,128)(2,1)}), bf16[32,3,128]{2,1,0:T(4,128)(2,1)S(1)}, u32[]{:S(2)}, u32[]{:S(2)}) async-start(bf16[32,3,128]{2,1,0:T(4,128)(2,1)} %stack.12), calls=%async_computation | async-start | bytes 65536 | tf_op jit(solution)/shard_map/all_to_all | solution.py:108
  50.6 6.3 %all-to-all-done = bf16[32,3,128]{2,1,0:T(4,128)(2,1)S(1)} async-done(((bf16[32,3,128]{2,1,0:T(4,128)(2,1)}), bf16[32,3,128]{2,1,0:T(4,128)(2,1)S(1)}, u32[]{:S(2)}, u32[]{:S(2)}) %all-to-all-start) | async-done | bytes 24608 | tf_op jit(solution)/shard_map/all_to_all | solution.py:108
  57.6 4.0 all-to-all-start.1
  61.6 38.5 %all-gather.5.cloned.1.call-done = bf16[128,4096]{1,0:T(8,128)(2,1)} async-done(((bf16[128,128]{1,0:T(8,128)(2,1)}), bf16[128,4096]{1,0:T(8,128)(2,1)}) %all-gather.5.cloned.1.call-update) | async-done | bytes 1048592 | tf_op jit(solution)/shard_map/all_gather | solution.py:113
  100.1 91.2 %while.56 = (s32[]{:T(128)}, f32[512,128]{0,1:T(8,128)S(1)}, bf16[3,512]{1,0:T(4,128)(2,1)S(1)}, bf16[3,4096]{1,0:T(4,128)(2,1)S(1)}, bf16[128,4096]{1,0:T(8,128...) while((s32[]{:T(128)}, f32[512,128]{0,1:T(8,128)S(1)}, bf16[3,512]{1,0:T(4,128)(2,1)S(1)}, ...), condition=%wide.region_3.4_spmd.clone, body=%wide.region_2.3_spmd.clone.sunk | while | flops 281283584 | bytes 2713769 | solution.py:75
  100.3 9.7 %fusion.110 = f32[512,128]{0,1:T(8,128)S(1)} fusion(f32[1024]{0:T(1024)S(1)} %bitcast.298, f32[512]{0:T(512)S(1)} %bitcast.324, f32[1024]{0:T(1024)S(1)} %bitcast.300, f32[512]{0:T(512)S(1)} %bitcast.322, f32[1024]{0:T(1024)S(1)} %bitcast.296, f32[512]{0:T(512)S(1)} %bitcast.320, bf16[128,4096]{1,0:T(8,128)(2,1)} %get-tuple-element.879, ...), kind=kOutput, calls=%fused_computation.79.clone.1 | convolution fusion | flops 140509184 | bytes 542724 | tf_op jit(solution)/shard_map/while/body/eval_jaxpr/dot_general | solution.py:36
  110.0 9.6 %fusion.111 = f32[512,128]{0,1:T(8,128)S(1)} fusion(f32[1024]{0:T(1024)S(1)} %bitcast.299, f32[512]{0:T(512)S(1)} %bitcast.325, f32[1024]{0:T(1024)S(1)} %bitcast.301, f32[512]{0:T(512)S(1)} %bitcast.323, f32[1024]{0:T(1024)S(1)} %bitcast.297, f32[512]{0:T(512)S(1)} %bitcast.321, bf16[128,4096]{1,0:T(8,128)(2,1)} %get-tuple-element.879, ...), kind=kOutput, calls=%fused_computation.78.clone.1 | convolution fusion | flops 140509184 | bytes 542724 | tf_op jit(solution)/shard_map/while/body/eval_jaxpr/dot_general | solution.py:35
  119.9 9.7 %fusion.110 = f32[512,128]{0,1:T(8,128)S(1)} fusion(f32[1024]{0:T(1024)S(1)} %bitcast.298, f32[512]{0:T(512)S(1)} %bitcast.324, f32[1024]{0:T(1024)S(1)} %bitcast.300, f32[512]{0:T(512)S(1)} %bitcast.322, f32[1024]{0:T(1024)S(1)} %bitcast.296, f32[512]{0:T(512)S(1)} %bitcast.320, bf16[128,4096]{1,0:T(8,128)(2,1)} %get-tuple-element.879, ...), kind=kOutput, calls=%fused_computation.79.clone.1 | convolution fusion | flops 140509184 | bytes 542724 | tf_op jit(solution)/shard_map/while/body/eval_jaxpr/dot_general | solution.py:36
  129.6 9.6 %fusion.111 = f32[512,128]{0,1:T(8,128)S(1)} fusion(f32[1024]{0:T(1024)S(1)} %bitcast.299, f32[512]{0:T(512)S(1)} %bitcast.325, f32[1024]{0:T(1024)S(1)} %bitcast.301, f32[512]{0:T(512)S(1)} %bitcast.323, f32[1024]{0:T(1024)S(1)} %bitcast.297, f32[512]{0:T(512)S(1)} %bitcast.321, bf16[128,4096]{1,0:T(8,128)(2,1)} %get-tuple-element.879, ...), kind=kOutput, calls=%fused_computation.78.clone.1 | convolution fusion | flops 140509184 | bytes 542724 | tf_op jit(solution)/shard_map/while/body/eval_jaxpr/dot_general | solution.py:35
  139.4 9.7 %fusion.110 = f32[512,128]{0,1:T(8,128)S(1)} fusion(f32[1024]{0:T(1024)S(1)} %bitcast.298, f32[512]{0:T(512)S(1)} %bitcast.324, f32[1024]{0:T(1024)S(1)} %bitcast.300, f32[512]{0:T(512)S(1)} %bitcast.322, f32[1024]{0:T(1024)S(1)} %bitcast.296, f32[512]{0:T(512)S(1)} %bitcast.320, bf16[128,4096]{1,0:T(8,128)(2,1)} %get-tuple-element.879, ...), kind=kOutput, calls=%fused_computation.79.clone.1 | convolution fusion | flops 140509184 | bytes 542724 | tf_op jit(solution)/shard_map/while/body/eval_jaxpr/dot_general | solution.py:36
  149.1 9.6 %fusion.111 = f32[512,128]{0,1:T(8,128)S(1)} fusion(f32[1024]{0:T(1024)S(1)} %bitcast.299, f32[512]{0:T(512)S(1)} %bitcast.325, f32[1024]{0:T(1024)S(1)} %bitcast.301, f32[512]{0:T(512)S(1)} %bitcast.323, f32[1024]{0:T(1024)S(1)} %bitcast.297, f32[512]{0:T(512)S(1)} %bitcast.321, bf16[128,4096]{1,0:T(8,128)(2,1)} %get-tuple-element.879, ...), kind=kOutput, calls=%fused_computation.78.clone.1 | convolution fusion | flops 140509184 | bytes 542724 | tf_op jit(solution)/shard_map/while/body/eval_jaxpr/dot_general | solution.py:35
  159.0 9.7 %fusion.110 = f32[512,128]{0,1:T(8,128)S(1)} fusion(f32[1024]{0:T(1024)S(1)} %bitcast.298, f32[512]{0:T(512)S(1)} %bitcast.324, f32[1024]{0:T(1024)S(1)} %bitcast.300, f32[512]{0:T(512)S(1)} %bitcast.322, f32[1024]{0:T(1024)S(1)} %bitcast.296, f32[512]{0:T(512)S(1)} %bitcast.320, bf16[128,4096]{1,0:T(8,128)(2,1)} %get-tuple-element.879, ...), kind=kOutput, calls=%fused_computation.79.clone.1 | convolution fusion | flops 140509184 | bytes 542724 | tf_op jit(solution)/shard_map/while/body/eval_jaxpr/dot_general | solution.py:36
  168.7 9.6 %fusion.111 = f32[512,128]{0,1:T(8,128)S(1)} fusion(f32[1024]{0:T(1024)S(1)} %bitcast.299, f32[512]{0:T(512)S(1)} %bitcast.325, f32[1024]{0:T(1024)S(1)} %bitcast.301, f32[512]{0:T(512)S(1)} %bitcast.323, f32[1024]{0:T(1024)S(1)} %bitcast.297, f32[512]{0:T(512)S(1)} %bitcast.321, bf16[128,4096]{1,0:T(8,128)(2,1)} %get-tuple-element.879, ...), kind=kOutput, calls=%fused_computation.78.clone.1 | convolution fusion | flops 140509184 | bytes 542724 | tf_op jit(solution)/shard_map/while/body/eval_jaxpr/dot_general | solution.py:35
  191.9 6.5 %all-to-all-start.2 = ((bf16[32,3,128]{2,1,0:T(4,128)(2,1)}), bf16[32,3,128]{2,1,0:T(4,128)(2,1)S(1)}, u32[]{:S(2)}, u32[]{:S(2)}) async-start(bf16[32,3,128]{2,1,0:T(4,128)(2,1)} %stack.14), calls=%async_computation.2 | async-start | bytes 65536 | tf_op jit(solution)/shard_map/all_to_all | solution.py:108
  198.4 91.0 %while.53 = (s32[]{:T(128)}, f32[512,128]{0,1:T(8,128)S(1)}, bf16[3,512]{1,0:T(4,128)(2,1)S(1)}, bf16[3,4096]{1,0:T(4,128)(2,1)S(1)}, bf16[128,4096]{1,0:T(8,128...) while((s32[]{:T(128)}, f32[512,128]{0,1:T(8,128)S(1)}, bf16[3,512]{1,0:T(4,128)(2,1)S(1)}, ...), condition=%wide.region_7.8_spmd, body=%wide.region_6.7_spmd.sunk | while | flops 281218048 | bytes 2713759 | solution.py:75
  198.5 9.7 %fusion.92 = f32[512,128]{0,1:T(8,128)S(1)} fusion(f32[1024]{0:T(1024)S(1)} %bitcast.304, f32[512]{0:T(512)S(1)} %bitcast.330, f32[1024]{0:T(1024)S(1)} %bitcast.306, f32[512]{0:T(512)S(1)} %bitcast.328, f32[1024]{0:T(1024)S(1)} %bitcast.302, f32[512]{0:T(512)S(1)} %bitcast.326, bf16[128,4096]{1,0:T(8,128)(2,1)} %get-tuple-element.906, ...), kind=kOutput, calls=%fused_computation.28.clone.1 | convolution fusion | flops 140509184 | bytes 542724 | tf_op jit(solution)/shard_map/while/body/eval_jaxpr/dot_general | solution.py:36
  208.2 9.6 %fusion.93 = f32[512,128]{0,1:T(8,128)S(1)} fusion(f32[1024]{0:T(1024)S(1)} %bitcast.305, f32[512]{0:T(512)S(1)} %bitcast.331, f32[1024]{0:T(1024)S(1)} %bitcast.307, f32[512]{0:T(512)S(1)} %bitcast.329, f32[1024]{0:T(1024)S(1)} %bitcast.303, f32[512]{0:T(512)S(1)} %bitcast.327, bf16[128,4096]{1,0:T(8,128)(2,1)} %get-tuple-element.906, ...), kind=kOutput, calls=%fused_computation.27.clone.1 | convolution fusion | flops 140509184 | bytes 542724 | tf_op jit(solution)/shard_map/while/body/eval_jaxpr/dot_general | solution.py:35
  218.0 9.7 %fusion.92 = f32[512,128]{0,1:T(8,128)S(1)} fusion(f32[1024]{0:T(1024)S(1)} %bitcast.304, f32[512]{0:T(512)S(1)} %bitcast.330, f32[1024]{0:T(1024)S(1)} %bitcast.306, f32[512]{0:T(512)S(1)} %bitcast.328, f32[1024]{0:T(1024)S(1)} %bitcast.302, f32[512]{0:T(512)S(1)} %bitcast.326, bf16[128,4096]{1,0:T(8,128)(2,1)} %get-tuple-element.906, ...), kind=kOutput, calls=%fused_computation.28.clone.1 | convolution fusion | flops 140509184 | bytes 542724 | tf_op jit(solution)/shard_map/while/body/eval_jaxpr/dot_general | solution.py:36
  227.7 9.6 %fusion.93 = f32[512,128]{0,1:T(8,128)S(1)} fusion(f32[1024]{0:T(1024)S(1)} %bitcast.305, f32[512]{0:T(512)S(1)} %bitcast.331, f32[1024]{0:T(1024)S(1)} %bitcast.307, f32[512]{0:T(512)S(1)} %bitcast.329, f32[1024]{0:T(1024)S(1)} %bitcast.303, f32[512]{0:T(512)S(1)} %bitcast.327, bf16[128,4096]{1,0:T(8,128)(2,1)} %get-tuple-element.906, ...), kind=kOutput, calls=%fused_computation.27.clone.1 | convolution fusion | flops 140509184 | bytes 542724 | tf_op jit(solution)/shard_map/while/body/eval_jaxpr/dot_general | solution.py:35
  237.6 9.7 %fusion.92 = f32[512,128]{0,1:T(8,128)S(1)} fusion(f32[1024]{0:T(1024)S(1)} %bitcast.304, f32[512]{0:T(512)S(1)} %bitcast.330, f32[1024]{0:T(1024)S(1)} %bitcast.306, f32[512]{0:T(512)S(1)} %bitcast.328, f32[1024]{0:T(1024)S(1)} %bitcast.302, f32[512]{0:T(512)S(1)} %bitcast.326, bf16[128,4096]{1,0:T(8,128)(2,1)} %get-tuple-element.906, ...), kind=kOutput, calls=%fused_computation.28.clone.1 | convolution fusion | flops 140509184 | bytes 542724 | tf_op jit(solution)/shard_map/while/body/eval_jaxpr/dot_general | solution.py:36
  247.3 9.6 %fusion.93 = f32[512,128]{0,1:T(8,128)S(1)} fusion(f32[1024]{0:T(1024)S(1)} %bitcast.305, f32[512]{0:T(512)S(1)} %bitcast.331, f32[1024]{0:T(1024)S(1)} %bitcast.307, f32[512]{0:T(512)S(1)} %bitcast.329, f32[1024]{0:T(1024)S(1)} %bitcast.303, f32[512]{0:T(512)S(1)} %bitcast.327, bf16[128,4096]{1,0:T(8,128)(2,1)} %get-tuple-element.906, ...), kind=kOutput, calls=%fused_computation.27.clone.1 | convolution fusion | flops 140509184 | bytes 542724 | tf_op jit(solution)/shard_map/while/body/eval_jaxpr/dot_general | solution.py:35
  257.1 9.7 %fusion.92 = f32[512,128]{0,1:T(8,128)S(1)} fusion(f32[1024]{0:T(1024)S(1)} %bitcast.304, f32[512]{0:T(512)S(1)} %bitcast.330, f32[1024]{0:T(1024)S(1)} %bitcast.306, f32[512]{0:T(512)S(1)} %bitcast.328, f32[1024]{0:T(1024)S(1)} %bitcast.302, f32[512]{0:T(512)S(1)} %bitcast.326, bf16[128,4096]{1,0:T(8,128)(2,1)} %get-tuple-element.906, ...), kind=kOutput, calls=%fused_computation.28.clone.1 | convolution fusion | flops 140509184 | bytes 542724 | tf_op jit(solution)/shard_map/while/body/eval_jaxpr/dot_general | solution.py:36
  266.8 9.6 %fusion.93 = f32[512,128]{0,1:T(8,128)S(1)} fusion(f32[1024]{0:T(1024)S(1)} %bitcast.305, f32[512]{0:T(512)S(1)} %bitcast.331, f32[1024]{0:T(1024)S(1)} %bitcast.307, f32[512]{0:T(512)S(1)} %bitcast.329, f32[1024]{0:T(1024)S(1)} %bitcast.303, f32[512]{0:T(512)S(1)} %bitcast.327, bf16[128,4096]{1,0:T(8,128)(2,1)} %get-tuple-element.906, ...), kind=kOutput, calls=%fused_computation.27.clone.1 | convolution fusion | flops 140509184 | bytes 542724 | tf_op jit(solution)/shard_map/while/body/eval_jaxpr/dot_general | solution.py:35
  290.1 9.8 %all-to-all-start.3 = ((bf16[32,3,128]{2,1,0:T(4,128)(2,1)}), bf16[32,3,128]{2,1,0:T(4,128)(2,1)S(1)}, u32[]{:S(2)}, u32[]{:S(2)}) async-start(bf16[32,3,128]{2,1,0:T(4,128)(2,1)} %stack.15), calls=%async_computation.3 | async-start | bytes 65536 | tf_op jit(solution)/shard_map/all_to_all | solution.py:108
  299.9 78.1 %while.54 = (s32[]{:T(128)}, f32[512,128]{0,1:T(8,128)S(1)}, bf16[3,512]{1,0:T(4,128)(2,1)S(1)}, bf16[3,4096]{1,0:T(4,128)(2,1)S(1)}, bf16[128,4096]{1,0:T(8,128...) while((s32[]{:T(128)}, f32[512,128]{0,1:T(8,128)S(1)}, bf16[3,512]{1,0:T(4,128)(2,1)S(1)}, ...), condition=%wide.region_11.12_spmd, body=%wide.region_10.11_spmd.sunk | while | flops 281218048 | bytes 2713759 | solution.py:75
  300.0 9.7 %fusion.98 = f32[512,128]{0,1:T(8,128)S(1)} fusion(f32[1024]{0:T(1024)S(1)} %bitcast.310, f32[512]{0:T(512)S(1)} %bitcast.336, f32[1024]{0:T(1024)S(1)} %bitcast.312, f32[512]{0:T(512)S(1)} %bitcast.334, f32[1024]{0:T(1024)S(1)} %bitcast.308, f32[512]{0:T(512)S(1)} %bitcast.332, bf16[128,4096]{1,0:T(8,128)(2,1)} %get-tuple-element.933, ...), kind=kOutput, calls=%fused_computation.45.clone.1 | convolution fusion | flops 140509184 | bytes 542724 | tf_op jit(solution)/shard_map/while/body/eval_jaxpr/dot_general | solution.py:36
  309.7 9.6 %fusion.99 = f32[512,128]{0,1:T(8,128)S(1)} fusion(f32[1024]{0:T(1024)S(1)} %bitcast.311, f32[512]{0:T(512)S(1)} %bitcast.337, f32[1024]{0:T(1024)S(1)} %bitcast.313, f32[512]{0:T(512)S(1)} %bitcast.335, f32[1024]{0:T(1024)S(1)} %bitcast.309, f32[512]{0:T(512)S(1)} %bitcast.333, bf16[128,4096]{1,0:T(8,128)(2,1)} %get-tuple-element.933, ...), kind=kOutput, calls=%fused_computation.44.clone.1 | convolution fusion | flops 140509184 | bytes 542724 | tf_op jit(solution)/shard_map/while/body/eval_jaxpr/dot_general | solution.py:35
  319.5 9.7 %fusion.98 = f32[512,128]{0,1:T(8,128)S(1)} fusion(f32[1024]{0:T(1024)S(1)} %bitcast.310, f32[512]{0:T(512)S(1)} %bitcast.336, f32[1024]{0:T(1024)S(1)} %bitcast.312, f32[512]{0:T(512)S(1)} %bitcast.334, f32[1024]{0:T(1024)S(1)} %bitcast.308, f32[512]{0:T(512)S(1)} %bitcast.332, bf16[128,4096]{1,0:T(8,128)(2,1)} %get-tuple-element.933, ...), kind=kOutput, calls=%fused_computation.45.clone.1 | convolution fusion | flops 140509184 | bytes 542724 | tf_op jit(solution)/shard_map/while/body/eval_jaxpr/dot_general | solution.py:36
  329.2 9.6 %fusion.99 = f32[512,128]{0,1:T(8,128)S(1)} fusion(f32[1024]{0:T(1024)S(1)} %bitcast.311, f32[512]{0:T(512)S(1)} %bitcast.337, f32[1024]{0:T(1024)S(1)} %bitcast.313, f32[512]{0:T(512)S(1)} %bitcast.335, f32[1024]{0:T(1024)S(1)} %bitcast.309, f32[512]{0:T(512)S(1)} %bitcast.333, bf16[128,4096]{1,0:T(8,128)(2,1)} %get-tuple-element.933, ...), kind=kOutput, calls=%fused_computation.44.clone.1 | convolution fusion | flops 140509184 | bytes 542724 | tf_op jit(solution)/shard_map/while/body/eval_jaxpr/dot_general | solution.py:35
  339.0 9.7 %fusion.98 = f32[512,128]{0,1:T(8,128)S(1)} fusion(f32[1024]{0:T(1024)S(1)} %bitcast.310, f32[512]{0:T(512)S(1)} %bitcast.336, f32[1024]{0:T(1024)S(1)} %bitcast.312, f32[512]{0:T(512)S(1)} %bitcast.334, f32[1024]{0:T(1024)S(1)} %bitcast.308, f32[512]{0:T(512)S(1)} %bitcast.332, bf16[128,4096]{1,0:T(8,128)(2,1)} %get-tuple-element.933, ...), kind=kOutput, calls=%fused_computation.45.clone.1 | convolution fusion | flops 140509184 | bytes 542724 | tf_op jit(solution)/shard_map/while/body/eval_jaxpr/dot_general | solution.py:36
  348.7 9.6 %fusion.99 = f32[512,128]{0,1:T(8,128)S(1)} fusion(f32[1024]{0:T(1024)S(1)} %bitcast.311, f32[512]{0:T(512)S(1)} %bitcast.337, f32[1024]{0:T(1024)S(1)} %bitcast.313, f32[512]{0:T(512)S(1)} %bitcast.335, f32[1024]{0:T(1024)S(1)} %bitcast.309, f32[512]{0:T(512)S(1)} %bitcast.333, bf16[128,4096]{1,0:T(8,128)(2,1)} %get-tuple-element.933, ...), kind=kOutput, calls=%fused_computation.44.clone.1 | convolution fusion | flops 140509184 | bytes 542724 | tf_op jit(solution)/shard_map/while/body/eval_jaxpr/dot_general | solution.py:35
  358.5 9.7 %fusion.98 = f32[512,128]{0,1:T(8,128)S(1)} fusion(f32[1024]{0:T(1024)S(1)} %bitcast.310, f32[512]{0:T(512)S(1)} %bitcast.336, f32[1024]{0:T(1024)S(1)} %bitcast.312, f32[512]{0:T(512)S(1)} %bitcast.334, f32[1024]{0:T(1024)S(1)} %bitcast.308, f32[512]{0:T(512)S(1)} %bitcast.332, bf16[128,4096]{1,0:T(8,128)(2,1)} %get-tuple-element.933, ...), kind=kOutput, calls=%fused_computation.45.clone.1 | convolution fusion | flops 140509184 | bytes 542724 | tf_op jit(solution)/shard_map/while/body/eval_jaxpr/dot_general | solution.py:36
  368.2 9.6 %fusion.99 = f32[512,128]{0,1:T(8,128)S(1)} fusion(f32[1024]{0:T(1024)S(1)} %bitcast.311, f32[512]{0:T(512)S(1)} %bitcast.337, f32[1024]{0:T(1024)S(1)} %bitcast.313, f32[512]{0:T(512)S(1)} %bitcast.335, f32[1024]{0:T(1024)S(1)} %bitcast.309, f32[512]{0:T(512)S(1)} %bitcast.333, bf16[128,4096]{1,0:T(8,128)(2,1)} %get-tuple-element.933, ...), kind=kOutput, calls=%fused_computation.44.clone.1 | convolution fusion | flops 140509184 | bytes 542724 | tf_op jit(solution)/shard_map/while/body/eval_jaxpr/dot_general | solution.py:35
  378.1 91.2 %while.55 = (s32[]{:T(128)}, f32[512,128]{0,1:T(8,128)S(1)}, bf16[3,512]{1,0:T(4,128)(2,1)S(1)}, bf16[3,4096]{1,0:T(4,128)(2,1)S(1)}, bf16[128,4096]{1,0:T(8,128...) while((s32[]{:T(128)}, f32[512,128]{0,1:T(8,128)S(1)}, bf16[3,512]{1,0:T(4,128)(2,1)S(1)}, ...), condition=%wide.region_15.16_spmd, body=%wide.region_14.15_spmd.sunk | while | flops 281218048 | bytes 2713759 | solution.py:75
  391.2 9.7 %fusion.104 = f32[512,128]{0,1:T(8,128)S(1)} fusion(f32[1024]{0:T(1024)S(1)} %bitcast.316, f32[512]{0:T(512)S(1)} %bitcast.342, f32[1024]{0:T(1024)S(1)} %bitcast.318, f32[512]{0:T(512)S(1)} %bitcast.340, f32[1024]{0:T(1024)S(1)} %bitcast.314, f32[512]{0:T(512)S(1)} %bitcast.338, bf16[128,4096]{1,0:T(8,128)(2,1)} %get-tuple-element.960, ...), kind=kOutput, calls=%fused_computation.62.clone.1 | convolution fusion | flops 140509184 | bytes 542724 | tf_op jit(solution)/shard_map/while/body/eval_jaxpr/dot_general | solution.py:36
  400.9 9.6 %fusion.105 = f32[512,128]{0,1:T(8,128)S(1)} fusion(f32[1024]{0:T(1024)S(1)} %bitcast.317, f32[512]{0:T(512)S(1)} %bitcast.343, f32[1024]{0:T(1024)S(1)} %bitcast.319, f32[512]{0:T(512)S(1)} %bitcast.341, f32[1024]{0:T(1024)S(1)} %bitcast.315, f32[512]{0:T(512)S(1)} %bitcast.339, bf16[128,4096]{1,0:T(8,128)(2,1)} %get-tuple-element.960, ...), kind=kOutput, calls=%fused_computation.61.clone.1 | convolution fusion | flops 140509184 | bytes 542724 | tf_op jit(solution)/shard_map/while/body/eval_jaxpr/dot_general | solution.py:35
  410.8 9.7 %fusion.104 = f32[512,128]{0,1:T(8,128)S(1)} fusion(f32[1024]{0:T(1024)S(1)} %bitcast.316, f32[512]{0:T(512)S(1)} %bitcast.342, f32[1024]{0:T(1024)S(1)} %bitcast.318, f32[512]{0:T(512)S(1)} %bitcast.340, f32[1024]{0:T(1024)S(1)} %bitcast.314, f32[512]{0:T(512)S(1)} %bitcast.338, bf16[128,4096]{1,0:T(8,128)(2,1)} %get-tuple-element.960, ...), kind=kOutput, calls=%fused_computation.62.clone.1 | convolution fusion | flops 140509184 | bytes 542724 | tf_op jit(solution)/shard_map/while/body/eval_jaxpr/dot_general | solution.py:36
  420.5 9.6 %fusion.105 = f32[512,128]{0,1:T(8,128)S(1)} fusion(f32[1024]{0:T(1024)S(1)} %bitcast.317, f32[512]{0:T(512)S(1)} %bitcast.343, f32[1024]{0:T(1024)S(1)} %bitcast.319, f32[512]{0:T(512)S(1)} %bitcast.341, f32[1024]{0:T(1024)S(1)} %bitcast.315, f32[512]{0:T(512)S(1)} %bitcast.339, bf16[128,4096]{1,0:T(8,128)(2,1)} %get-tuple-element.960, ...), kind=kOutput, calls=%fused_computation.61.clone.1 | convolution fusion | flops 140509184 | bytes 542724 | tf_op jit(solution)/shard_map/while/body/eval_jaxpr/dot_general | solution.py:35
  430.3 9.7 %fusion.104 = f32[512,128]{0,1:T(8,128)S(1)} fusion(f32[1024]{0:T(1024)S(1)} %bitcast.316, f32[512]{0:T(512)S(1)} %bitcast.342, f32[1024]{0:T(1024)S(1)} %bitcast.318, f32[512]{0:T(512)S(1)} %bitcast.340, f32[1024]{0:T(1024)S(1)} %bitcast.314, f32[512]{0:T(512)S(1)} %bitcast.338, bf16[128,4096]{1,0:T(8,128)(2,1)} %get-tuple-element.960, ...), kind=kOutput, calls=%fused_computation.62.clone.1 | convolution fusion | flops 140509184 | bytes 542724 | tf_op jit(solution)/shard_map/while/body/eval_jaxpr/dot_general | solution.py:36
  440.0 9.6 %fusion.105 = f32[512,128]{0,1:T(8,128)S(1)} fusion(f32[1024]{0:T(1024)S(1)} %bitcast.317, f32[512]{0:T(512)S(1)} %bitcast.343, f32[1024]{0:T(1024)S(1)} %bitcast.319, f32[512]{0:T(512)S(1)} %bitcast.341, f32[1024]{0:T(1024)S(1)} %bitcast.315, f32[512]{0:T(512)S(1)} %bitcast.339, bf16[128,4096]{1,0:T(8,128)(2,1)} %get-tuple-element.960, ...), kind=kOutput, calls=%fused_computation.61.clone.1 | convolution fusion | flops 140509184 | bytes 542724 | tf_op jit(solution)/shard_map/while/body/eval_jaxpr/dot_general | solution.py:35
  449.8 9.7 %fusion.104 = f32[512,128]{0,1:T(8,128)S(1)} fusion(f32[1024]{0:T(1024)S(1)} %bitcast.316, f32[512]{0:T(512)S(1)} %bitcast.342, f32[1024]{0:T(1024)S(1)} %bitcast.318, f32[512]{0:T(512)S(1)} %bitcast.340, f32[1024]{0:T(1024)S(1)} %bitcast.314, f32[512]{0:T(512)S(1)} %bitcast.338, bf16[128,4096]{1,0:T(8,128)(2,1)} %get-tuple-element.960, ...), kind=kOutput, calls=%fused_computation.62.clone.1 | convolution fusion | flops 140509184 | bytes 542724 | tf_op jit(solution)/shard_map/while/body/eval_jaxpr/dot_general | solution.py:36
  459.5 9.6 %fusion.105 = f32[512,128]{0,1:T(8,128)S(1)} fusion(f32[1024]{0:T(1024)S(1)} %bitcast.317, f32[512]{0:T(512)S(1)} %bitcast.343, f32[1024]{0:T(1024)S(1)} %bitcast.319, f32[512]{0:T(512)S(1)} %bitcast.341, f32[1024]{0:T(1024)S(1)} %bitcast.315, f32[512]{0:T(512)S(1)} %bitcast.339, bf16[128,4096]{1,0:T(8,128)(2,1)} %get-tuple-element.960, ...), kind=kOutput, calls=%fused_computation.61.clone.1 | convolution fusion | flops 140509184 | bytes 542724 | tf_op jit(solution)/shard_map/while/body/eval_jaxpr/dot_general | solution.py:35
  470.2 74.9 %all-reduce.2.cloned.1.call-done = f32[512,128]{1,0:T(8,128)} async-done(((f32[512,128]{1,0:T(8,128)}), f32[512,128]{1,0:T(8,128)}) %all-reduce.2.cloned.1.call-update) | async-done | bytes 262160 | tf_op jit(solution)/shard_map/psum | solution.py:116
  546.3 7.5 %collective-permute-start.1 = (f32[8,128]{1,0:T(8,128)S(1)}, f32[8,128]{1,0:T(8,128)S(1)}, u32[]{:S(2)}, u32[]{:S(2)}) collective-permute-start(f32[8,128]{1,0:T(8,128)S(1)} %get-tuple-element.580), channel_id=1, source_target_pairs={{8,0},{16,8},{24,16},{32,24},{40,32},{48,40},{56,48},{64,56},{72,6... | collective-permute-start | bytes 12296 | tf_op jit(solution)/shard_map/ppermute | solution.py:20
  553.8 4.2 collective-permute-start
  568.9 1.6 multiply_add_fusion
  (197 shorter events, 35.4 us)
Async XLA Ops:
  6.5 93.5 %all-gather.5.cloned.1.call-start = ((), (), s32[]{:S(2)}) async-start(), calls=%async_computation.4 | async-start | bytes 1081344 | tf_op jit(solution)/shard_map/all_gather | solution.py:113
  17.7 5.0 copy-start.6
  17.7 5.0 copy-start.7
  17.7 5.0 copy-start.8
  17.7 5.1 copy-start.5
  23.6 174.8 %all-gather.7.cloned.1.call-start = ((), (), s32[]{:S(2)}) async-start(), calls=%async_computation.5 | async-start | bytes 1081344 | tf_op jit(solution)/shard_map/all_gather | solution.py:113
  26.8 273.1 %all-gather.9.cloned.1.call-start = ((), (), s32[]{:S(2)}) async-start(), calls=%async_computation.6 | async-start | bytes 1081344 | tf_op jit(solution)/shard_map/all_gather | solution.py:113
  29.5 4.4 copy-start.4
  33.2 66.9 %copy-start = (bf16[3,512]{1,0:T(4,128)(2,1)S(1)}, bf16[3,512]{1,0:T(4,128)(2,1)}, u32[]{:S(2)}) copy-start(bf16[3,512]{1,0:T(4,128)(2,1)} %param.20) | copy-start | bytes 9220
  34.6 22.4 %all-to-all-start = ((bf16[32,3,128]{2,1,0:T(4,128)(2,1)}), bf16[32,3,128]{2,1,0:T(4,128)(2,1)S(1)}, u32[]{:S(2)}, u32[]{:S(2)}) async-start(bf16[32,3,128]{2,1,0:T(4,128)(2,1)} %stack.12), calls=%async_computation | async-start | bytes 65536 | tf_op jit(solution)/shard_map/all_to_all | solution.py:108
  47.3 330.7 %all-gather.11.cloned.1.call-start = ((), (), s32[]{:S(2)}) async-start(), calls=%async_computation.7 | async-start | bytes 1081344 | tf_op jit(solution)/shard_map/all_gather | solution.py:113
  57.6 133.7 %all-to-all-start.1 = ((bf16[32,3,128]{2,1,0:T(4,128)(2,1)}), bf16[32,3,128]{2,1,0:T(4,128)(2,1)S(1)}, u32[]{:S(2)}, u32[]{:S(2)}) async-start(bf16[32,3,128]{2,1,0:T(4,128)(2,1)} %stack.13), calls=%async_computation.1 | async-start | bytes 65536 | tf_op jit(solution)/shard_map/all_to_all | solution.py:108
  191.9 97.5 %all-to-all-start.2 = ((bf16[32,3,128]{2,1,0:T(4,128)(2,1)}), bf16[32,3,128]{2,1,0:T(4,128)(2,1)S(1)}, u32[]{:S(2)}, u32[]{:S(2)}) async-start(bf16[32,3,128]{2,1,0:T(4,128)(2,1)} %stack.14), calls=%async_computation.2 | async-start | bytes 65536 | tf_op jit(solution)/shard_map/all_to_all | solution.py:108
  290.1 88.0 %all-to-all-start.3 = ((bf16[32,3,128]{2,1,0:T(4,128)(2,1)}), bf16[32,3,128]{2,1,0:T(4,128)(2,1)S(1)}, u32[]{:S(2)}, u32[]{:S(2)}) async-start(bf16[32,3,128]{2,1,0:T(4,128)(2,1)} %stack.15), calls=%async_computation.3 | async-start | bytes 65536 | tf_op jit(solution)/shard_map/all_to_all | solution.py:108
  299.8 245.3 %all-reduce.2.cloned.1.call-start = ((), (), s32[]{:S(2)}) async-start(), calls=%async_computation.8 | async-start | bytes 524288 | tf_op jit(solution)/shard_map/psum | solution.py:116
  378.0 92.1 %copy-start.9 = (f32[512]{0:T(512)S(1)}, f32[512]{0:T(512)}, u32[]{:S(2)}) copy-start(f32[512]{0:T(512)} %param.21) | copy-start | bytes 6148
  378.1 92.1 %copy-start.3 = (f32[8,512]{1,0:T(8,128)S(1)}, f32[8,512]{1,0:T(8,128)}, u32[]{:S(2)}) copy-start(f32[8,512]{1,0:T(8,128)} %param.30) | copy-start | bytes 49156
  469.3 88.8 %copy-start.2 = (s32[8]{0:T(128)S(1)}, s32[8]{0:T(128)}, u32[]{:S(2)}) copy-start(s32[8]{0:T(128)} %param.31) | copy-start | bytes 100
  545.2 23.8 %copy-start.1 = (f32[512,128]{1,0:T(8,128)S(1)}, f32[512,128]{1,0:T(8,128)}, u32[]{:S(2)}) copy-start(f32[512,128]{1,0:T(8,128)} %all-reduce.2.cloned.1.call-done) | copy-start | bytes 786436
  546.3 22.5 %collective-permute-start.1 = (f32[8,128]{1,0:T(8,128)S(1)}, f32[8,128]{1,0:T(8,128)S(1)}, u32[]{:S(2)}, u32[]{:S(2)}) collective-permute-start(f32[8,128]{1,0:T(8,128)S(1)} %get-tuple-element.580), channel_id=1, source_target_pairs={{8,0},{16,8},{24,16},{32,24},{40,32},{48,40},{56,48},{64,56},{72,6... | collective-permute-start | bytes 12296 | tf_op jit(solution)/shard_map/ppermute | solution.py:20
  553.8 15.1 %collective-permute-start = (f32[8,128]{1,0:T(8,128)S(1)}, f32[8,128]{1,0:T(8,128)S(1)}, u32[]{:S(2)}, u32[]{:S(2)}) collective-permute-start(f32[8,128]{1,0:T(8,128)S(1)} %get-tuple-element.579), channel_id=1, source_target_pairs={{0,8},{8,16},{16,24},{24,32},{32,40},{40,48},{48,56},{56,64},{64,7... | collective-permute-start | bytes 12296 | tf_op jit(solution)/shard_map/ppermute | solution.py:17
Sparse Core Ops, SparseCore 0:
  23.7 76.3 all-gather.4
  102.6 69.9 all-gather.6
  175.2 69.9 all-gather.8
  247.6 69.9 all-gather.10
  470.3 74.8 all-reduce.1
